TPU v7x, 512 devices: a whole 4x4x16 slice. The times are simulated.
512 devices in a mesh: expert: 128 (over x, z_lo, y), dp: 4 (over z_hi, core).
Axes of the slice: x: 4, y: 4, z: 16 (z_hi: 2, z_lo: 8; z = z_hi * 8 + z_lo), core: 2. Of those that a mesh axis runs over, the one named last changes fastest.
Arguments:
- tokens: bfloat16 [8192, 2048], P(('expert', 'dp')), may hold values from -6 to 6
- cotangent: bfloat16 [8192, 2048], P(('expert', 'dp')), may hold values from -6 to 6
- route_ids: int32 [8192, 8], P(('expert', 'dp')), may hold values from 0 to 127, all different within a row; in each aligned block of 16 rows (0 to 15, 16 to 31, ...) at most 2 rows name the same one
- route_gates: bfloat16 [8192, 8], P(('expert', 'dp')), may hold values from 0.019897461 to 0.5
- gate_up: bfloat16 [128, 2048, 1536], P('expert', 'dp'), may hold values from -0.125 to 0.125
- down: bfloat16 [128, 2048, 768], P('expert', 'dp'), may hold values from -6 to 6
- moment1: bfloat16 [128, 2048, 768], P('expert', 'dp'), may hold values from -4 to 4
- moment2: bfloat16 [128, 2048, 768], P('expert', 'dp'), may hold values from 0.049804688 to 0.5
- placement: int32 [128], replicated, may hold values from 0 to 127, each once
Outputs:
- rollout_down: bfloat16 [128, 2048, 768], P('expert', None, 'dp')
Inputs may be any that keep to these rules, and one draw needn't show every extreme that they name: `route_ids`: each row names 8 different experts; within the rows of one device no expert is named more than 2 times, a bound that some block reaches. `placement`: each expert exactly once.
All inputs are finite; a program needn't handle non-finite values.
Results may differ from a plain program's by a relative error of at most 0.003.
Values may be sent and summed in bfloat16 or wider, within the bound.
A program may use at most 64 MiB of HBM per device.

v0:
```python
import jax
import jax.numpy as jnp
from jax import lax
from jax.sharding import Mesh, PartitionSpec as P

OPT_STEP = 2
BETA_ONE = 0.9
BETA_TWO = 0.95
ADAM_EPS = 1e-08
LEARN_RATE = 0.25
DP = ("zh", "core")
PLANE = ("x", "y")
EXPERT = ("x", "zl", "y")
CAP = 2
META = 128
contract_rows = (((0,), (0,)), ((), ()))


def pickers(meta, blocks, block_rows, top):
    plane = lax.axis_size(PLANE)
    wide = meta.shape[0]
    ids = meta[:, :top].astype(jnp.int32)
    gates = meta[:, top : 2 * top].astype(jnp.float32)
    place = jnp.arange(plane, dtype=jnp.int32)
    y_size = lax.axis_size("y")
    wanted = (
        place // y_size * lax.axis_size("zl") + lax.axis_index("zl")
    ) * y_size + place % y_size
    match = (ids[:, :, None] == wanted).astype(jnp.float32)
    hits = jnp.sum(match, axis=1)
    worth = jnp.sum(match * gates[:, :, None], axis=1)
    token = jnp.arange(wide, dtype=jnp.int32)
    own_block = token // block_rows
    before = (
        (own_block[:, None] == own_block[None, :]) & (token[None, :] < token[:, None])
    ).astype(jnp.bfloat16)
    earlier = jnp.dot(before, hits.astype(jnp.bfloat16), preferred_element_type=jnp.float32)
    row = jnp.arange(plane * blocks * CAP, dtype=jnp.int32)
    row_place = row // (blocks * CAP)
    spread = (row_place[:, None] == place[None, :]).astype(jnp.bfloat16)
    take = lambda v: lax.dot_general(
        spread, v.astype(jnp.bfloat16), (((1,), (1,)), ((), ())), preferred_element_type=jnp.float32
    )
    here = (row // CAP % blocks)[:, None] == own_block[None, :]
    slot = jnp.where(hits > 0, earlier, -1.0)
    chosen = here & (take(slot) == (row % CAP)[:, None].astype(jnp.float32))
    one_hot = chosen.astype(jnp.bfloat16)
    return (one_hot, jnp.where(chosen, take(worth), 0.0).astype(jnp.bfloat16))


def shards(tokens, cotangent, route_ids, route_gates, gate_up, down, moment1, moment2, placement):
    tok_rows, width = tokens.shape
    top = route_ids.shape[1]
    hidden_units = down.shape[2]
    groups = lax.axis_size(DP)
    line = lax.axis_size("zl")
    plane = lax.axis_size(PLANE)
    experts = lax.axis_size(EXPERT)
    share = width // groups
    bf16 = jnp.bfloat16
    meta = jnp.concatenate(
        [route_ids.astype(bf16), route_gates, jnp.zeros((tok_rows, META - 2 * top), bf16)], axis=1
    )
    tok_pack = lax.all_gather(jnp.concatenate([tokens, meta], axis=1), "zl", axis=0, tiled=True)
    cot_parts = cotangent.reshape(tok_rows, groups, share).transpose(1, 0, 2)
    cot_parts = jnp.concatenate(
        [cot_parts, jnp.broadcast_to(meta[None], (groups, tok_rows, META))], axis=2
    )
    cot_parts = lax.all_to_all(cot_parts, DP, split_axis=0, concat_axis=0, tiled=True)
    cot_pack = lax.all_gather(
        cot_parts.reshape(groups * tok_rows, share + META), "zl", axis=0, tiled=True
    )
    gate_up, cot_pack, tok_pack = lax.optimization_barrier((gate_up, cot_pack, tok_pack))
    weights = lax.all_gather(gate_up[0], DP, axis=0, tiled=True)
    tok_pick, _ = pickers(tok_pack[:, width:], line, tok_rows, top)
    rows = jnp.dot(tok_pick, tok_pack[:, :width], preferred_element_type=jnp.float32).astype(bf16)
    rows = lax.all_to_all(
        rows.reshape(plane, line * CAP, width), PLANE, split_axis=0, concat_axis=0, tiled=True
    ).reshape(plane * line * CAP, width)
    _, cot_pick = pickers(cot_pack[:, share:], line * groups, tok_rows, top)
    scaled = jnp.dot(cot_pick, cot_pack[:, :share], preferred_element_type=jnp.float32).astype(bf16)
    scaled = lax.all_to_all(
        scaled.reshape(plane, line * groups * CAP, share),
        PLANE,
        split_axis=0,
        concat_axis=0,
        tiled=True,
    )
    scaled = scaled.reshape(plane * line, groups, CAP, share).transpose(1, 0, 2, 3)
    scaled = scaled.reshape(groups * plane * line * CAP, share)
    pre = jnp.dot(rows, weights, preferred_element_type=jnp.float32)
    hidden = (jax.nn.silu(pre[:, :hidden_units]) * pre[:, hidden_units:]).astype(bf16)
    hidden = lax.all_gather(hidden, DP, axis=0, tiled=True)
    grad = lax.dot_general(scaled, hidden, contract_rows, preferred_element_type=jnp.float32)
    correct_one = 1.0 - BETA_ONE**OPT_STEP
    correct_two = 1.0 - BETA_TWO**OPT_STEP
    first = BETA_ONE * moment1[0].astype(jnp.float32) + (1.0 - BETA_ONE) * grad
    second = BETA_TWO * moment2[0].astype(jnp.float32) + (1.0 - BETA_TWO) * grad * grad
    direction = first / correct_one / (jnp.sqrt(second / correct_two) + ADAM_EPS)
    updated = (down[0].astype(jnp.float32) - LEARN_RATE * direction).astype(bf16)
    block_cols = hidden_units // groups
    piece_rows = share // experts
    pieces = updated.reshape(experts, piece_rows, groups, block_cols).transpose(0, 2, 1, 3)
    pieces = pieces.reshape(experts * groups, piece_rows * block_cols)
    spread = lax.all_to_all(pieces, EXPERT + DP, split_axis=0, concat_axis=0, tiled=True)
    spread = spread.reshape(experts, groups * piece_rows * block_cols)
    picked = jnp.take(spread, placement, axis=0)
    landed = lax.all_to_all(picked, EXPERT, split_axis=0, concat_axis=0, tiled=True)
    landed = landed.reshape(experts, groups, piece_rows, block_cols).transpose(1, 0, 2, 3)
    return landed.reshape(1, width, block_cols)


def solution(mesh):
    grid = Mesh(mesh.devices.reshape(4, 8, 4, 2, 2), EXPERT + DP)
    every = P(EXPERT + DP, None)
    owned = P(EXPERT, DP, None)
    placed = (every, every, every, every, owned, owned, owned, owned, P())
    return jax.shard_map(
        shards, mesh=grid, in_specs=placed, out_specs=P(EXPERT, None, DP), check_vma=False
    )
```

profile of v0, /device:TPU:1, one launch (start us, length us, event | category | flops | bytes accessed | tf_op | source)
XLA Modules:
  0.0 495.7 jit_solution(6455398087655121743)
XLA Ops:
  6.5 0.8 copy.84
  7.3 0.8 copy.83
  8.1 0.9 reshape.250
  8.9 0.1 pad_maximum_fusion.1
  9.1 0.6 copy.85
  9.7 16.6 %all-to-all-start = ((bf16[4,16,640]{2,1,0:T(8,128)(2,1)}), bf16[4,16,640]{2,1,0:T(8,128)(2,1)S(1)}, u32[]{:S(2)}, u32[]{:S(2)}) async-start(bf16[4,16,640]{2,1,0:T(8,128)(2,1)} %copy.85), calls=%async_computation | async-start | bytes 163840 | tf_op jit(solution)/shard_map/all_to_all | solution.py:69
  26.3 0.9 concatenate.12
  27.2 42.3 %all_gather.13 = bf16[128,2176]{1,0:T(8,128)(2,1)S(1)} all-gather(bf16[16,2176]{1,0:T(8,128)(2,1)S(1)} %concatenate.12), channel_id=1, replica_groups=mesh['x'=4,'zl'=8,'y'=4,'zh'=2,'core'=2] {'zl'}, dimensions={0}, use_global_device_ids=true | all-gather | bytes 626688 | tf_op jit(solution)/shard_map/all_gather | solution.py:64
  69.5 43.4 %all_gather.12 = bf16[512,640]{1,0:T(8,128)(2,1)S(1)} all-gather(bf16[64,640]{1,0:T(8,128)(2,1)S(1)} %bitcast.41), channel_id=1, replica_groups=mesh['x'=4,'zl'=8,'y'=4,'zh'=2,'core'=2] {'zl'}, dimensions={0}, use_global_device_ids=true | all-gather | bytes 737280 | tf_op jit(solution)/shard_map/all_gather | solution.py:70
  113.1 0.3 copy.90
  113.4 0.1 convert_reduce_fusion
  113.5 0.2 fusion.14
  113.7 0.6 convolution_convert_fusion
  114.3 18.3 %all_to_all.31 = bf16[16,16,2048]{2,1,0:T(8,128)(2,1)S(1)} all-to-all(bf16[16,16,2048]{2,1,0:T(8,128)(2,1)S(1)} %bitcast.36), channel_id=1, replica_groups=mesh['x'=4,'zl'=8,'y'=4,'zh'=2,'core'=2] {'x','y'}, dimensions={0} | all-to-all | bytes 2097152 | tf_op jit(solution)/shard_map/all_to_all | solution.py:77
  132.7 156.0 %all-gather.6.cloned.1.call-done = bf16[1,2048,1536]{2,1,0:T(8,128)(2,1)} async-done(((bf16[1,512,1536]{2,1,0:T(8,128)(2,1)}), bf16[1,2048,1536]{2,1,0:T(8,128)(2,1)}) %all-gather.6.cloned.1.call-update) | async-done | bytes 6291472 | tf_op jit(solution)/shard_map/all_gather | solution.py:74
  288.6 4.6 fusion
  293.2 1.0 fusion.24
  294.2 0.3 copy.87
  294.5 0.1 fusion.32
  294.6 0.7 fusion.13
  295.3 2.0 convolution_convert_fusion.1
  297.4 19.4 %all_to_all.32 = bf16[16,64,512]{2,1,0:T(8,128)(2,1)S(1)} all-to-all(bf16[16,64,512]{2,1,0:T(8,128)(2,1)} %bitcast.39), channel_id=1, replica_groups=mesh['x'=4,'zl'=8,'y'=4,'zh'=2,'core'=2] {'x','y'}, dimensions={0} | all-to-all | bytes 2097152 | tf_op jit(solution)/shard_map/all_to_all | solution.py:82
  316.7 0.4 reshape.253
  317.1 0.7 copy.89
  317.9 0.4 reshape.254
  318.3 37.2 %all-gather.4.cloned.1.call-done = bf16[1024,768]{1,0:T(8,128)(2,1)} async-done(((bf16[256,768]{1,0:T(8,128)(2,1)}), bf16[1024,768]{1,0:T(8,128)(2,1)}) %all-gather.4.cloned.1.call-update) | async-done | bytes 1572880 | tf_op jit(solution)/shard_map/all_gather | solution.py:93
  355.6 3.9 fusion.10
  359.5 0.9 reshape.257
  360.4 0.4 copy.91
  360.8 1.8 all_to_all.25
  362.6 0.6 broadcast.427
  363.2 5.5 %reduce.1 = bf16[512,768]{1,0:T(8,128)(2,1)S(1)} reduce(bf16[512,1,768]{2,1,0:T(2,128)(2,1)S(1)} %all_to_all.25, bf16[]{:T(256)} %broadcast.427), dimensions={1}, to_apply=%all_to_all.25.reduce_sub_computation | reduce | bytes 1572866 | tf_op jit(solution)/shard_map/all_to_all | solution.py:105
  368.7 1.1 reshape.273
  369.7 10.5 %all-to-all-start.3 = ((bf16[512,2,384]{2,1,0:T(2,128)(2,1)}), bf16[512,2,384]{2,1,0:T(2,128)(2,1)S(1)}, u32[]{:S(2)}, u32[]{:S(2)}) async-start(bf16[512,2,384]{2,1,0:T(2,128)(2,1)} %reshape.273), calls=%async_computation.3 | async-start | bytes 1572864 | tf_op jit(solution)/shard_map/all_to_all | solution.py:105
  380.2 46.2 %all-to-all-done.3 = bf16[512,2,384]{2,1,0:T(2,128)(2,1)S(1)} async-done(((bf16[512,2,384]{2,1,0:T(2,128)(2,1)}), bf16[512,2,384]{2,1,0:T(2,128)(2,1)S(1)}, u32[]{:S(2)}, u32[]{:S(2)}) %all-to-all-start.3) | async-done | bytes 786464 | tf_op jit(solution)/shard_map/all_to_all | solution.py:105
  426.5 0.6 reshape.274
  427.1 5.0 %reduce = bf16[512,768]{1,0:T(8,128)(2,1)S(1)} reduce(bf16[512,1,768]{2,1,0:T(2,128)(2,1)S(1)} %reshape.274, bf16[]{:T(256)} %constant.215), dimensions={1}, to_apply=%all_to_all.23.reduce_sub_computation | reduce | bytes 1572866 | tf_op jit(solution)/shard_map/all_to_all | solution.py:105
  432.1 0.5 reshape.258
  432.6 1.0 gather_fusion
  433.6 0.1 bitcast_select_fusion
  433.8 1.2 reduce.2
  435.0 0.6 reshape.275
  435.6 48.3 %all_to_all.33 = bf16[128,2,1536]{2,1,0:T(2,128)(2,1)S(1)} all-to-all(bf16[128,2,1536]{2,1,0:T(2,128)(2,1)S(1)} %reshape.275), channel_id=1, replica_groups=mesh['x'=4,'zl'=8,'y'=4,'zh'=2,'core'=2] {'x','zl','y'}, dimensions={0} | all-to-all | bytes 1572864 | tf_op jit(solution)/shard_map/all_to_all | solution.py:108
  483.8 0.6 reshape.276
  484.5 1.8 copy.94
  486.3 0.7 copy.95
  487.0 0.7 reshape.260
  487.6 1.2 copy.96
  (25 shorter events, 0.2 us)
Async XLA Ops:
  9.7 59.8 %all-to-all-start = ((bf16[4,16,640]{2,1,0:T(8,128)(2,1)}), bf16[4,16,640]{2,1,0:T(8,128)(2,1)S(1)}, u32[]{:S(2)}, u32[]{:S(2)}) async-start(bf16[4,16,640]{2,1,0:T(8,128)(2,1)} %copy.85), calls=%async_computation | async-start | bytes 163840 | tf_op jit(solution)/shard_map/all_to_all | solution.py:69
  26.3 262.3 %all-gather.6.cloned.1.call-start = ((), (), s32[]{:S(2)}) async-start(), calls=%async_computation.6 | async-start | bytes 7864320 | tf_op jit(solution)/shard_map/all_gather | solution.py:74
  113.0 242.6 %all-gather.4.cloned.1.call-start = ((), (), s32[]{:S(2)}) async-start(), calls=%async_computation.5 | async-start | bytes 1966080 | tf_op jit(solution)/shard_map/all_gather | solution.py:93
  317.9 37.7 %copy-start = (bf16[1,512,768]{2,1,0:T(8,128)(2,1)S(1)}, bf16[1,512,768]{2,1,0:T(8,128)(2,1)}, u32[]{:S(2)}) copy-start(bf16[1,512,768]{2,1,0:T(8,128)(2,1)} %param.16) | copy-start | bytes 2359300
  368.6 11.6 %copy-start.1 = (s32[128]{0:T(128)S(1)}, s32[128]{0:T(128)}, u32[]{:S(2)}) copy-start(s32[128]{0:T(128)} %param.17) | copy-start | bytes 1540
  369.7 56.8 %all-to-all-start.3 = ((bf16[512,2,384]{2,1,0:T(2,128)(2,1)}), bf16[512,2,384]{2,1,0:T(2,128)(2,1)S(1)}, u32[]{:S(2)}, u32[]{:S(2)}) async-start(bf16[512,2,384]{2,1,0:T(2,128)(2,1)} %reshape.273), calls=%async_computation.3 | async-start | bytes 1572864 | tf_op jit(solution)/shard_map/all_to_all | solution.py:105
Sparse Core Ops, SparseCore 0:
  113.1 175.4 all-gather.5
  294.3 61.2 all-gather.3
where the time goes:
time: 496 us
  waiting for transfers between devices  239 us (48%)
  blocking collectives  172 us (35%)
  starting transfers between devices  27.1 us (5%)
  local copies, waits for them, and re-layouts  18.6 us (4%)
  between operations  13.7 us (3%)
  other arithmetic  13.2 us (3%)
  matrix products  12 us (2%)
    all_gather x1, waiting for transfers between devices, shards(): weights = lax.all_gather(gate_up[0], DP, axis=0, tiled=True)  156 us
    all_to_all x1, blocking collectives, shards(): lax.all_to_all(picked, EXPERT, split_axis=0, concat_axis=0, tiled=True)  48.3 us
    all_to_all x1, waiting for transfers between devices, shards(): lax.all_to_all(pieces, EXPERT + DP, split_axis=0, concat_axis=0, tiled=True)  46.2 us
    all_gather x1, blocking collectives, shards(): lax.all_gather(cot_parts.reshape(groups * tok_rows, share + META), 'zl',...  43.4 us
    all_gather x1, blocking collectives, shards(): lax.all_gather(jnp.concatenate([tokens, meta], axis=1), 'zl', axis=0, til...  42.3 us
    all_gather x1, waiting for transfers between devices, shards(): hidden = lax.all_gather(hidden, DP, axis=0, tiled=True)  37.2 us
    all_to_all x1, blocking collectives, shards(): lax.all_to_all(scaled.reshape(plane, line * groups * CAP, share), PLANE,...  19.4 us
    all_to_all x1, blocking collectives, shards(): lax.all_to_all(rows.reshape(plane, line * CAP, width), PLANE, split_axis=...  18.3 us
  transfers between devices with their start and end apart: 4, of which 3 were waited for; matrix products, arithmetic and copies ran while one was open for 1% of the time, Pallas kernels for 0%

commit v1 on v0

--- a/solution.py
+++ b/solution.py
@@ -61,7 +61,12 @@
     meta = jnp.concatenate(
         [route_ids.astype(bf16), route_gates, jnp.zeros((tok_rows, META - 2 * top), bf16)], axis=1
     )
-    tok_pack = lax.all_gather(jnp.concatenate([tokens, meta], axis=1), "zl", axis=0, tiled=True)
+    tok_pack = jnp.concatenate(
+        lax.all_to_all(
+            jnp.stack([jnp.concatenate([tokens, meta], axis=1)] * lax.axis_size("zl")), "zl", 0, 0
+        ),
+        axis=0,
+    )
     cot_parts = cotangent.reshape(tok_rows, groups, share).transpose(1, 0, 2)
     cot_parts = jnp.concatenate(
         [cot_parts, jnp.broadcast_to(meta[None], (groups, tok_rows, META))], axis=2

time: 496 us -> 469 us (0.946)
  blocking collectives: 172 us -> 138 us
    all_gather x1 -> x0, blocking collectives: 42.3 us -> none  [shards(): lax.all_gather(jnp.concatenate([tokens, meta], axis=1), 'zl', axis=0, til...]
    all_to_all x1, waiting for transfers between devices: 0.01 us -> 11.1 us  [shards(): lax.all_to_all(cot_parts, DP, split_axis=0, concat_axis=0, tiled=True)]
    all_gather x1, waiting for transfers between devices: 156 us -> 146 us  [shards(): weights = lax.all_gather(gate_up[0], DP, axis=0, tiled=True)]
    all_gather x1, blocking collectives: 43.4 us -> 51.8 us  [shards(): lax.all_gather(cot_parts.reshape(groups * tok_rows, share + META), 'zl',...]
  transfers between devices with their start and end apart: 4 -> 5, of which waited for: 3 -> 4; matrix products, arithmetic and copies ran while one was open for 1% -> 1% of each run, Pallas kernels for 0% -> 0%
where the time goes in v1:
time: 469 us; the launch traced here: 468 us
  waiting for transfers between devices  241 us (51%)
  blocking collectives  138 us (29%)
  starting transfers between devices  31.9 us (7%)
  local copies, waits for them, and re-layouts  18.7 us (4%)
  between operations  13.7 us (3%)
  other arithmetic  13.6 us (3%)
  matrix products  12 us (3%)
    all_gather x1, waiting for transfers between devices, shards(): weights = lax.all_gather(gate_up[0], DP, axis=0, tiled=True)  146 us
    all_gather x1, blocking collectives, shards(): lax.all_gather(cot_parts.reshape(groups * tok_rows, share + META), 'zl',...  51.8 us
    all_to_all x1, blocking collectives, shards(): lax.all_to_all(picked, EXPERT, split_axis=0, concat_axis=0, tiled=True)  48.3 us
    all_to_all x1, waiting for transfers between devices, shards(): lax.all_to_all(pieces, EXPERT + DP, split_axis=0, concat_axis=0, tiled=True)  46.2 us
    all_gather x1, waiting for transfers between devices, shards(): hidden = lax.all_gather(hidden, DP, axis=0, tiled=True)  37.2 us
    all_to_all x1, blocking collectives, shards(): lax.all_to_all(scaled.reshape(plane, line * groups * CAP, share), PLANE,...  19.4 us
    all_to_all x1, blocking collectives, shards(): lax.all_to_all(rows.reshape(plane, line * CAP, width), PLANE, split_axis=...  18.3 us
    all_to_all x1, starting transfers between devices, shards(): lax.all_to_all(cot_parts, DP, split_axis=0, concat_axis=0, tiled=True)  16.6 us
  transfers between devices with their start and end apart: 5, of which 4 were waited for; matrix products, arithmetic and copies ran while one was open for 1% of the time, Pallas kernels for 0%

profile of v1, /device:TPU:1, one launch (start us, length us, event | category | flops | bytes accessed | tf_op | source)
XLA Modules:
  0.0 468.4 jit_solution(11811742979448897754)
XLA Ops:
  6.5 0.7 convert_element_type.86
  7.3 0.8 copy.102
  8.1 0.9 reshape.255
  9.1 0.6 copy.103
  9.7 16.6 %all-to-all-start = ((bf16[4,16,640]{2,1,0:T(8,128)(2,1)}), bf16[4,16,640]{2,1,0:T(8,128)(2,1)S(1)}, u32[]{:S(2)}, u32[]{:S(2)}) async-start(bf16[4,16,640]{2,1,0:T(8,128)(2,1)} %copy.103), calls=%async_computation | async-start | bytes 163840 | tf_op jit(solution)/shard_map/all_to_all | solution.py:74
  26.3 0.9 concatenate.12
  27.2 11.1 %all-to-all-done = bf16[4,16,640]{2,1,0:T(8,128)(2,1)S(1)} async-done(((bf16[4,16,640]{2,1,0:T(8,128)(2,1)}), bf16[4,16,640]{2,1,0:T(8,128)(2,1)S(1)}, u32[]{:S(2)}, u32[]{:S(2)}) %all-to-all-start) | async-done | bytes 81952 | tf_op jit(solution)/shard_map/all_to_all | solution.py:74
  38.3 0.8 stack.2
  39.2 4.7 %all-to-all-start.1 = ((bf16[8,16,2176]{2,1,0:T(8,128)(2,1)}), bf16[8,16,2176]{2,1,0:T(8,128)(2,1)S(1)}, u32[]{:S(2)}, u32[]{:S(2)}) async-start(bf16[8,16,2176]{2,1,0:T(8,128)(2,1)} %stack.2), calls=%async_computation.1 | async-start | bytes 1114112 | tf_op jit(solution)/shard_map/all_to_all | solution.py:65
  44.0 51.8 %all_gather.9 = bf16[512,640]{1,0:T(8,128)(2,1)S(1)} all-gather(bf16[64,640]{1,0:T(8,128)(2,1)S(1)} %bitcast.44), channel_id=1, replica_groups=mesh['x'=4,'zl'=8,'y'=4,'zh'=2,'core'=2] {'zl'}, dimensions={0}, use_global_device_ids=true | all-gather | bytes 737280 | tf_op jit(solution)/shard_map/all_gather | solution.py:75
  95.9 0.3 copy.109
  96.4 0.2 fusion.14
  96.6 0.6 convolution_convert_fusion
  97.2 18.3 %all_to_all.36 = bf16[16,16,2048]{2,1,0:T(8,128)(2,1)S(1)} all-to-all(bf16[16,16,2048]{2,1,0:T(8,128)(2,1)S(1)} %bitcast.39), channel_id=1, replica_groups=mesh['x'=4,'zl'=8,'y'=4,'zh'=2,'core'=2] {'x','y'}, dimensions={0} | all-to-all | bytes 2097152 | tf_op jit(solution)/shard_map/all_to_all | solution.py:82
  115.5 146.2 %all-gather.6.cloned.1.call-done = bf16[1,2048,1536]{2,1,0:T(8,128)(2,1)} async-done(((bf16[1,512,1536]{2,1,0:T(8,128)(2,1)}), bf16[1,2048,1536]{2,1,0:T(8,128)(2,1)}) %all-gather.6.cloned.1.call-update) | async-done | bytes 6291472 | tf_op jit(solution)/shard_map/all_gather | solution.py:79
  261.7 4.6 fusion
  266.2 1.0 fusion.24
  267.3 0.3 copy.106
  267.6 0.1 fusion.32
  267.7 0.7 fusion.13
  268.4 2.0 convolution_convert_fusion.1
  270.4 19.4 %all_to_all.37 = bf16[16,64,512]{2,1,0:T(8,128)(2,1)S(1)} all-to-all(bf16[16,64,512]{2,1,0:T(8,128)(2,1)} %bitcast.42), channel_id=1, replica_groups=mesh['x'=4,'zl'=8,'y'=4,'zh'=2,'core'=2] {'x','y'}, dimensions={0} | all-to-all | bytes 2097152 | tf_op jit(solution)/shard_map/all_to_all | solution.py:87
  289.8 0.4 reshape.259
  290.2 0.7 copy.108
  291.0 0.4 reshape.260
  291.4 37.2 %all-gather.4.cloned.1.call-done = bf16[1024,768]{1,0:T(8,128)(2,1)} async-done(((bf16[256,768]{1,0:T(8,128)(2,1)}), bf16[1024,768]{1,0:T(8,128)(2,1)}) %all-gather.4.cloned.1.call-update) | async-done | bytes 1572880 | tf_op jit(solution)/shard_map/all_gather | solution.py:98
  328.6 3.9 fusion.10
  332.5 0.9 reshape.263
  333.4 0.4 copy.110
  333.9 1.8 all_to_all.29
  335.6 0.5 broadcast.429
  336.1 5.3 %reduce.1 = bf16[512,768]{1,0:T(8,128)(2,1)S(1)} reduce(bf16[512,1,768]{2,1,0:T(2,128)(2,1)S(1)} %all_to_all.29, bf16[]{:T(256)} %broadcast.429), dimensions={1}, to_apply=%all_to_all.29.reduce_sub_computation | reduce | bytes 1572866 | tf_op jit(solution)/shard_map/all_to_all | solution.py:110
  341.5 1.1 reshape.279
  342.6 10.5 %all-to-all-start.4 = ((bf16[512,2,384]{2,1,0:T(2,128)(2,1)}), bf16[512,2,384]{2,1,0:T(2,128)(2,1)S(1)}, u32[]{:S(2)}, u32[]{:S(2)}) async-start(bf16[512,2,384]{2,1,0:T(2,128)(2,1)} %reshape.279), calls=%async_computation.4 | async-start | bytes 1572864 | tf_op jit(solution)/shard_map/all_to_all | solution.py:110
  353.1 46.2 %all-to-all-done.4 = bf16[512,2,384]{2,1,0:T(2,128)(2,1)S(1)} async-done(((bf16[512,2,384]{2,1,0:T(2,128)(2,1)}), bf16[512,2,384]{2,1,0:T(2,128)(2,1)S(1)}, u32[]{:S(2)}, u32[]{:S(2)}) %all-to-all-start.4) | async-done | bytes 786464 | tf_op jit(solution)/shard_map/all_to_all | solution.py:110
  399.3 0.6 reshape.280
  400.0 5.0 %reduce = bf16[512,768]{1,0:T(8,128)(2,1)S(1)} reduce(bf16[512,1,768]{2,1,0:T(2,128)(2,1)S(1)} %reshape.280, bf16[]{:T(256)} %constant.215), dimensions={1}, to_apply=%all_to_all.27.reduce_sub_computation | reduce | bytes 1572866 | tf_op jit(solution)/shard_map/all_to_all | solution.py:110
  404.9 0.5 reshape.264
  405.4 1.0 gather_fusion
  406.5 0.1 bitcast_select_fusion
  406.6 1.1 reduce.2
  407.7 0.6 reshape.281
  408.3 48.3 %all_to_all.38 = bf16[128,2,1536]{2,1,0:T(2,128)(2,1)S(1)} all-to-all(bf16[128,2,1536]{2,1,0:T(2,128)(2,1)S(1)} %reshape.281), channel_id=1, replica_groups=mesh['x'=4,'zl'=8,'y'=4,'zh'=2,'core'=2] {'x','zl','y'}, dimensions={0} | all-to-all | bytes 1572864 | tf_op jit(solution)/shard_map/all_to_all | solution.py:113
  456.6 0.6 reshape.282
  457.2 1.8 copy.113
  459.0 0.7 copy.114
  459.7 0.7 reshape.266
  460.4 1.2 copy.115
  (27 shorter events, 0.5 us)
Async XLA Ops:
  9.7 28.6 %all-to-all-start = ((bf16[4,16,640]{2,1,0:T(8,128)(2,1)}), bf16[4,16,640]{2,1,0:T(8,128)(2,1)S(1)}, u32[]{:S(2)}, u32[]{:S(2)}) async-start(bf16[4,16,640]{2,1,0:T(8,128)(2,1)} %copy.103), calls=%async_computation | async-start | bytes 163840 | tf_op jit(solution)/shard_map/all_to_all | solution.py:74
  39.2 56.6 %all-to-all-start.1 = ((bf16[8,16,2176]{2,1,0:T(8,128)(2,1)}), bf16[8,16,2176]{2,1,0:T(8,128)(2,1)S(1)}, u32[]{:S(2)}, u32[]{:S(2)}) async-start(bf16[8,16,2176]{2,1,0:T(8,128)(2,1)} %stack.2), calls=%async_computation.1 | async-start | bytes 1114112 | tf_op jit(solution)/shard_map/all_to_all | solution.py:65
  43.9 217.7 %all-gather.6.cloned.1.call-start = ((), (), s32[]{:S(2)}) async-start(), calls=%async_computation.7 | async-start | bytes 7864320 | tf_op jit(solution)/shard_map/all_gather | solution.py:79
  95.8 232.8 %all-gather.4.cloned.1.call-start = ((), (), s32[]{:S(2)}) async-start(), calls=%async_computation.6 | async-start | bytes 1966080 | tf_op jit(solution)/shard_map/all_gather | solution.py:98
  290.9 37.7 %copy-start = (bf16[1,512,768]{2,1,0:T(8,128)(2,1)S(1)}, bf16[1,512,768]{2,1,0:T(8,128)(2,1)}, u32[]{:S(2)}) copy-start(bf16[1,512,768]{2,1,0:T(8,128)(2,1)} %param.16) | copy-start | bytes 2359300
  341.5 11.6 %copy-start.1 = (s32[128]{0:T(128)S(1)}, s32[128]{0:T(128)}, u32[]{:S(2)}) copy-start(s32[128]{0:T(128)} %param.17) | copy-start | bytes 1540
  342.6 56.8 %all-to-all-start.4 = ((bf16[512,2,384]{2,1,0:T(2,128)(2,1)}), bf16[512,2,384]{2,1,0:T(2,128)(2,1)S(1)}, u32[]{:S(2)}, u32[]{:S(2)}) async-start(bf16[512,2,384]{2,1,0:T(2,128)(2,1)} %reshape.279), calls=%async_computation.4 | async-start | bytes 1572864 | tf_op jit(solution)/shard_map/all_to_all | solution.py:110
Sparse Core Ops, SparseCore 0:
  95.9 165.6 all-gather.5
  267.4 61.2 all-gather.3
